TPU v7x, 32 devices: a whole 2x2x4 slice. The times are simulated.
32 devices in a mesh: pole: 4 (over x, core), grid: 8 (over z, y).
Axes of the slice: x: 2, y: 2, z: 4, core: 2. Of those that a mesh axis runs over, the one named last changes fastest.
Arguments:
- anc_inv: bfloat16 [4, 1536, 1536], P('pole', 'grid'), may hold values from -6 to 6
- factor_cols: bfloat16 [4, 8, 2, 256, 256], P('pole', 'grid'), may hold values from -0.25 to 0.25
- diag_inv: bfloat16 [4, 8, 256, 256], P('pole', 'grid'), may hold values from -6 to 6
- intersection: bfloat16 [8, 256, 256], P('grid'), may hold values from -0.0234375 to 0.0234375
- pole_w: float32 [4], P('pole'), may hold values from 0.5 to 2
- pole_z: float32 [4], P('pole'), may hold values from -2 to -0.5
- ancestors: int32 [8, 2], P('grid'), may hold values from 0 to 5, as said below
- counts: int32 [8], P('grid'), may hold values from 1 to 2
- hpattern: int32 [8, 2], P('grid'), may hold values 0 or 1
- siesta_of: int32 [2048], P('grid'), may hold values from 0 to 2047, as said below
- supernode_of: int32 [2048], P('grid'), may hold values from 0 to 2047, as said below
Outputs:
- density: bfloat16 [2048, 768], P('grid', 'pole')
- energy: bfloat16 [2048, 768], P('grid', 'pole')
- electrons: float32 [], replicated
Inputs may be any that keep to these rules, and one draw needn't show every extreme that they name: `ancestors`: the 2 entries of a row are distinct. `siesta_of`: A permutation; supernode K's 256 orbitals go to each block-column owner (index // 256) at most 32 times, and exactly 32 times to some owner. `supernode_of`: the inverse permutation of siesta_of.
All inputs are finite; a program needn't handle non-finite values. No bound on the sum of `hpattern` on one device may be relied on, other than what follows from the above.
Results may differ from a plain program's by a relative error of at most 0.001.
Values may be sent and summed in bfloat16 or wider, within the bound.
No kernel may reach another device: no remote copies, remote signals or barrier semaphores. Data moves between devices by JAX's collectives and lax.ppermute only.
A program may use at most 64 MiB of HBM per device.

v0:
```python
import jax
import jax.numpy as jnp
from jax import lax
from jax.sharding import PartitionSpec as P


def body(
    anc_inv,
    factor_cols,
    diag_inv,
    intersection,
    pole_w,
    pole_z,
    ancestors,
    counts,
    hpattern,
    siesta_of,
    supernode_of,
):
    width = diag_inv.shape[-1]
    anc_count = anc_inv.shape[2] // width
    blk_count = ancestors.shape[1]
    select = (ancestors[0][:, None] == jnp.arange(anc_count)[None, :]).astype(jnp.bfloat16)
    live_mask = (jnp.arange(blk_count) < counts[0]).astype(jnp.bfloat16)
    lower_cols = (factor_cols[0, 0] * live_mask[:, None, None]).reshape(blk_count * width, width)
    gathered = lax.all_gather(anc_inv[0], "grid", axis=0, tiled=True)
    row_count = gathered.shape[0]
    picked = jnp.einsum(
        "rnw,mn->rmw",
        gathered.reshape(row_count, anc_count, width),
        select,
        preferred_element_type=jnp.float32,
    ).astype(jnp.bfloat16)
    product = jnp.dot(
        picked.reshape(row_count, blk_count * width), lower_cols, preferred_element_type=jnp.float32
    )
    blocks = product.reshape(anc_count, width, width)
    chosen = -jnp.sum(select.astype(jnp.float32)[:, :, None, None] * blocks[None], axis=1)
    diag_block = diag_inv[0, 0].astype(jnp.float32) - jnp.dot(
        lower_cols.astype(jnp.float32).T,
        chosen.reshape(blk_count * width, width),
        precision=lax.Precision.HIGHEST,
        preferred_element_type=jnp.float32,
    )
    masked = chosen * hpattern[0].astype(jnp.float32)[:, None, None]
    stacked = jnp.concatenate([diag_block[None], masked], axis=0)
    cols_rows = stacked.transpose(2, 0, 1).reshape(width, (blk_count + 1) * width)
    own_count = pole_w[0] * jnp.sum(diag_block * intersection[0].astype(jnp.float32))
    electrons = lax.psum(own_count, ("pole", "grid"))
    dens_term = pole_w[0] * cols_rows
    energy_term = pole_z[0] * cols_rows
    dens_part, energy_part = (
        lax.psum_scatter(dens_term, "pole", scatter_dimension=1, tiled=True),
        lax.psum_scatter(energy_term, "pole", scatter_dimension=1, tiled=True),
    )
    row_width = dens_part.shape[1]
    grid_count = lax.axis_size("grid")
    slot_cap = (width + grid_count - 1) // grid_count
    positions = jnp.arange(width)
    dest_owner = siesta_of // width
    same_dest = dest_owner[:, None] == dest_owner[None, :]
    earlier = positions[:, None] > positions[None, :]
    send_rank = jnp.sum((same_dest & earlier).astype(jnp.int32), axis=1)
    send_slot = dest_owner * slot_cap + send_rank
    placement = (jnp.arange(grid_count * slot_cap)[:, None] == send_slot[None, :]).astype(
        jnp.bfloat16
    )
    send_dens = (
        jnp.dot(placement, dens_part.astype(jnp.bfloat16), preferred_element_type=jnp.float32)
        .astype(jnp.bfloat16)
        .reshape(grid_count, slot_cap, row_width)
    )
    send_energy = (
        jnp.dot(placement, energy_part.astype(jnp.bfloat16), preferred_element_type=jnp.float32)
        .astype(jnp.bfloat16)
        .reshape(grid_count, slot_cap, row_width)
    )
    recv_dens, recv_energy = (
        lax.all_to_all(send_dens, "grid", split_axis=0, concat_axis=0, tiled=True),
        lax.all_to_all(send_energy, "grid", split_axis=0, concat_axis=0, tiled=True),
    )
    source_dev = supernode_of // width
    same_source = source_dev[:, None] == source_dev[None, :]
    before = supernode_of[None, :] < supernode_of[:, None]
    recv_rank = jnp.sum((same_source & before).astype(jnp.int32), axis=1)
    recv_slot = source_dev * slot_cap + recv_rank
    pickup = (recv_slot[:, None] == jnp.arange(grid_count * slot_cap)[None, :]).astype(jnp.bfloat16)
    density = jnp.dot(
        pickup,
        recv_dens.reshape(grid_count * slot_cap, row_width),
        preferred_element_type=jnp.float32,
    ).astype(jnp.bfloat16)
    energy = jnp.dot(
        pickup,
        recv_energy.reshape(grid_count * slot_cap, row_width),
        preferred_element_type=jnp.float32,
    ).astype(jnp.bfloat16)
    return (density, energy, electrons)


def solution(mesh):
    placed = (
        P("pole", "grid", None),
        P("pole", "grid", None, None, None),
        P("pole", "grid", None, None),
        P("grid", None, None),
        P("pole"),
        P("pole"),
        P("grid", None),
        P("grid"),
        P("grid", None),
        P("grid"),
        P("grid"),
    )
    return jax.shard_map(
        body,
        mesh=mesh,
        in_specs=placed,
        out_specs=(P("grid", "pole"), P("grid", "pole"), P()),
        check_vma=False,
    )
```

profile of v0, /device:TPU:0, one launch (start us, length us, event | category | flops | bytes accessed | tf_op | source)
XLA Modules:
  0.0 190.2 jit_solution(11743723445649057235)
XLA Ops:
  7.2 0.7 all-gather.3.cloned.1.call-update
  9.9 0.7 convert_bitcast_fusion
  10.6 0.7 fusion.16
  11.3 1.0 broadcast_multiply_fusion
  12.3 79.9 %all-gather.3.cloned.1.call-done = bf16[1,1536,1536]{2,1,0:T(8,128)(2,1)} async-done(((bf16[1,192,1536]{2,1,0:T(8,128)(2,1)}), bf16[1,1536,1536]{2,1,0:T(8,128)(2,1)}) %all-gather.3.cloned.1.call-update) | async-done | bytes 4718608 | tf_op jit(solution)/shard_map/all_gather | solution.py:26
  92.2 6.7 %copy.25 = bf16[1,1536,1536]{1,2,0:T(8,128)(2,1)} copy(bf16[1,1536,1536]{2,1,0:T(8,128)(2,1)} %all-gather.3.cloned.1.call-done) | data formatting | bytes 9437184 | tf_op jit(solution)/shard_map/all_gather | solution.py:26
  99.0 8.7 %copy.26 = bf16[1536,6,256]{2,1,0:T(8,128)(2,1)} copy(bf16[1536,6,256]{0,2,1:T(8,128)(2,1)} %bitcast.50) | data formatting | bytes 9437184 | tf_op jit(solution)/shard_map/reshape | solution.py:30
  107.6 4.6 %fusion = bf16[1536,2,256]{2,1,0:T(2,128)(2,1)S(1)} fusion(bf16[1536,6,256]{2,1,0:T(8,128)(2,1)} %copy.26, s32[2]{0:T(128)S(1)} %bitcast.58), kind=kOutput, calls=%fused_computation.2 | convolution fusion | flops 10223628 | bytes 6291464 | tf_op jit(solution)/shard_map/rnw,mn->rmw/dot_general | solution.py:28
  112.3 1.1 reshape.95
  113.4 0.6 fusion.18
  114.4 1.2 fusion.5
  115.5 1.3 fusion.2
  116.9 0.7 reduce-scatter.3.cloned.1.call-update
  118.7 38.6 %psum.7 = f32[]{:T(128)} all-reduce(f32[]{:T(128)S(6)} %mul.94), channel_id=1, replica_groups=mesh['pole'=4,'grid'=8] {'pole','grid'}, use_global_device_ids=true, to_apply=%region_6.7 | all-reduce | flops 1 | bytes 8 | tf_op jit(solution)/shard_map/psum | solution.py:49
  157.4 1.1 convolution_convert_fusion.2
  158.5 0.8 copy.29
  159.3 5.5 %all-to-all-start.1 = ((bf16[8,32,192]{2,1,0:T(8,128)(2,1)}), bf16[8,32,192]{2,1,0:T(8,128)(2,1)S(1)}, u32[]{:S(2)}, u32[]{:S(2)}) async-start(bf16[8,32,192]{2,1,0:T(8,128)(2,1)} %bitcast.20), calls=%async_computation.3 | async-start | bytes 262144 | tf_op jit(solution)/shard_map/all_to_all | solution.py:80
  164.8 1.1 convolution_convert_fusion.4
  165.9 0.8 copy.28
  166.7 5.4 %all-to-all-done.1 = bf16[8,32,192]{2,1,0:T(8,128)(2,1)S(1)} async-done(((bf16[8,32,192]{2,1,0:T(8,128)(2,1)}), bf16[8,32,192]{2,1,0:T(8,128)(2,1)S(1)}, u32[]{:S(2)}, u32[]{:S(2)}) %all-to-all-start.1) | async-done | bytes 98336 | tf_op jit(solution)/shard_map/all_to_all | solution.py:80
  172.1 3.4 %all-to-all-start = ((bf16[8,32,192]{2,1,0:T(8,128)(2,1)}), bf16[8,32,192]{2,1,0:T(8,128)(2,1)S(1)}, u32[]{:S(2)}, u32[]{:S(2)}) async-start(bf16[8,32,192]{2,1,0:T(8,128)(2,1)} %bitcast.15), calls=%async_computation.1 | async-start | bytes 262144 | tf_op jit(solution)/shard_map/all_to_all | solution.py:79
  175.5 0.9 convolution_convert_fusion.1
  176.4 6.3 %all-to-all-done = bf16[8,32,192]{2,1,0:T(8,128)(2,1)S(1)} async-done(((bf16[8,32,192]{2,1,0:T(8,128)(2,1)}), bf16[8,32,192]{2,1,0:T(8,128)(2,1)S(1)}, u32[]{:S(2)}, u32[]{:S(2)}) %all-to-all-start) | async-done | bytes 98336 | tf_op jit(solution)/shard_map/all_to_all | solution.py:79
  182.8 0.9 convolution_convert_fusion.3
  (27 shorter events, 1.0 us)
Async XLA Ops:
  7.2 85.1 %all-gather.3.cloned.1.call-start = ((), (), s32[]{:S(2)}) async-start(), calls=%async_computation.6 | async-start | bytes 5308416 | tf_op jit(solution)/shard_map/all_gather | solution.py:26
  7.9 149.5 %reduce-scatter.5.cloned.1.call-start = ((), (), s32[]{:S(2)}) async-start(), calls=%async_computation.5 | async-start | bytes 983040 | tf_op jit(solution)/shard_map/reduce_scatter | solution.py:54
  99.0 8.7 %copy-start.5 = (s32[1,2]{1,0:T(1,128)S(1)}, s32[1,2]{1,0:T(1,128)}, u32[]{:S(2)}) copy-start(s32[1,2]{1,0:T(1,128)} %param.17) | copy-start | bytes 28
  113.3 1.0 copy-start
  113.3 1.0 copy-start.1
  113.3 1.0 copy-start.2
  114.2 3.4 %copy-start.4 = (s32[256]{0:T(256)S(1)}, s32[256]{0:T(256)}, u32[]{:S(2)}) copy-start(s32[256]{0:T(256)} %param.20) | copy-start | bytes 3076
  114.2 3.6 %copy-start.3 = (s32[256]{0:T(256)S(1)}, s32[256]{0:T(256)}, u32[]{:S(2)}) copy-start(s32[256]{0:T(256)} %param.21) | copy-start | bytes 3076
  116.9 47.9 %reduce-scatter.3.cloned.1.call-start = ((), (), s32[]{:S(2)}) async-start(), calls=%async_computation.4 | async-start | bytes 983040 | tf_op jit(solution)/shard_map/reduce_scatter | solution.py:53
  159.3 12.8 %all-to-all-start.1 = ((bf16[8,32,192]{2,1,0:T(8,128)(2,1)}), bf16[8,32,192]{2,1,0:T(8,128)(2,1)S(1)}, u32[]{:S(2)}, u32[]{:S(2)}) async-start(bf16[8,32,192]{2,1,0:T(8,128)(2,1)} %bitcast.20), calls=%async_computation.3 | async-start | bytes 262144 | tf_op jit(solution)/shard_map/all_to_all | solution.py:80
  172.1 10.7 %all-to-all-start = ((bf16[8,32,192]{2,1,0:T(8,128)(2,1)}), bf16[8,32,192]{2,1,0:T(8,128)(2,1)S(1)}, u32[]{:S(2)}, u32[]{:S(2)}) async-start(bf16[8,32,192]{2,1,0:T(8,128)(2,1)} %bitcast.15), calls=%async_computation.1 | async-start | bytes 262144 | tf_op jit(solution)/shard_map/all_to_all | solution.py:79
Sparse Core Ops, SparseCore 0:
  10.2 82.0 all-gather.2
  117.0 21.6 reduce-scatter.4
  141.2 23.1 reduce-scatter.2
where the time goes:
time: 191 us; the launch traced here: 190 us
  waiting for transfers between devices  93.1 us (49%)
  blocking collectives  38.6 us (20%)
  local copies, waits for them, and re-layouts  18 us (9%)
  between operations  16.5 us (9%)
  matrix products  10.5 us (5%)
  starting transfers between devices  8.97 us (5%)
  other arithmetic  4.55 us (2%)
    all_gather x1, waiting for transfers between devices, body(): gathered = lax.all_gather(anc_inv[0], 'grid', axis=0, tiled=True)  79.9 us
    psum x1, blocking collectives, body(): electrons = lax.psum(own_count, ('pole', 'grid'))  38.6 us
    reshape x1, local copies, waits for them, and re-layouts, body(): gathered.reshape(row_count, anc_count, width)  8.66 us
    all_gather x1, local copies, waits for them, and re-layouts, body(): gathered = lax.all_gather(anc_inv[0], 'grid', axis=0, tiled=True)  6.72 us
    all_to_all x1, waiting for transfers between devices, body(): lax.all_to_all(send_dens, 'grid', split_axis=0, concat_axis=0, tiled=True)  6.35 us
    all_to_all x1, starting transfers between devices, body(): lax.all_to_all(send_energy, 'grid', split_axis=0, concat_axis=0, tiled=True)  5.48 us
    all_to_all x1, waiting for transfers between devices, body(): lax.all_to_all(send_energy, 'grid', split_axis=0, concat_axis=0, tiled=True)  5.42 us
    dot_general x1, matrix products, body(): jnp.einsum('rnw,mn->rmw', gathered.reshape(row_count, anc_count, width),...  4.62 us
  transfers between devices with their start and end apart: 5, of which 3 were waited for; matrix products, arithmetic and copies ran while one was open for 4% of the time, Pallas kernels for 0%

commit v1 on v0

--- a/solution.py
+++ b/solution.py
@@ -2,6 +2,18 @@
 import jax.numpy as jnp
 from jax import lax
 from jax.sharding import PartitionSpec as P
+
+
+def gather_by_bits(shard, axis, dim):
+    ways, here = (lax.axis_size(axis), lax.axis_index(axis))
+    grown, reach = (shard, 1)
+    while reach < ways:
+        theirs = lax.ppermute(grown, axis, [(d, d ^ reach) for d in range(ways)])
+        mine_first = jnp.concatenate([grown, theirs], axis=dim)
+        theirs_first = jnp.concatenate([theirs, grown], axis=dim)
+        grown = jnp.where(here & reach == 0, mine_first, theirs_first)
+        reach = 2 * reach
+    return grown
 
 
 def body(
@@ -23,7 +35,7 @@
     select = (ancestors[0][:, None] == jnp.arange(anc_count)[None, :]).astype(jnp.bfloat16)
     live_mask = (jnp.arange(blk_count) < counts[0]).astype(jnp.bfloat16)
     lower_cols = (factor_cols[0, 0] * live_mask[:, None, None]).reshape(blk_count * width, width)
-    gathered = lax.all_gather(anc_inv[0], "grid", axis=0, tiled=True)
+    gathered = gather_by_bits(anc_inv[0], "grid", 0)
     row_count = gathered.shape[0]
     picked = jnp.einsum(
         "rnw,mn->rmw",

time: 191 us -> 251 us (1.31)
  waiting for transfers between devices: 93.1 us -> 140 us
  starting transfers between devices: 8.97 us -> 17 us
  other arithmetic: 4.55 us -> 8.87 us
    ppermute x0 -> x3, waiting for transfers between devices: none -> 128 us  [gather_by_bits(): theirs = lax.ppermute(grown, axis, [(d, d ^ reach) for d in range(ways)])]
    all_gather x1 -> x0, waiting for transfers between devices: 79.9 us -> none  [body(): gathered = lax.all_gather(anc_inv[0], 'grid', axis=0, tiled=True)]
    concatenate x0 -> x4, local copies, waits for them, and re-layouts: none -> 9.7 us  [gather_by_bits(): mine_first = jnp.concatenate([grown, theirs], axis=dim)]
    reshape x1 -> x0, local copies, waits for them, and re-layouts: 8.66 us -> none  [body(): gathered.reshape(row_count, anc_count, width)]
    ppermute x0 -> x3, starting transfers between devices: none -> 7.45 us  [gather_by_bits(): theirs = lax.ppermute(grown, axis, [(d, d ^ reach) for d in range(ways)])]
    all_gather x1 -> x0, local copies, waits for them, and re-layouts: 6.72 us -> none  [body(): gathered = lax.all_gather(anc_inv[0], 'grid', axis=0, tiled=True)]
    select_n x0 -> x4, other arithmetic: none -> 5.87 us  [gather_by_bits(): grown = jnp.where(here & reach == 0, mine_first, theirs_first)]
  transfers between devices with their start and end apart: 5 -> 7, of which waited for: 3 -> 6; matrix products, arithmetic and copies ran while one was open for 4% -> 6% of each run, Pallas kernels for 0% -> 0%
where the time goes in v1:
time: 251 us
  waiting for transfers between devices  140 us (56%)
  blocking collectives  39.4 us (16%)
  starting transfers between devices  17 us (7%)
  local copies, waits for them, and re-layouts  16.8 us (7%)
  between operations  16.8 us (7%)
  matrix products  11.5 us (5%)
  other arithmetic  8.87 us (4%)
    ppermute x3, waiting for transfers between devices, gather_by_bits(): theirs = lax.ppermute(grown, axis, [(d, d ^ reach) for d in range(ways)])  128 us
    psum x1, blocking collectives, body(): electrons = lax.psum(own_count, ('pole', 'grid'))  39.4 us
    concatenate x4, local copies, waits for them, and re-layouts, gather_by_bits(): mine_first = jnp.concatenate([grown, theirs], axis=dim)  9.7 us
    ppermute x3, starting transfers between devices, gather_by_bits(): theirs = lax.ppermute(grown, axis, [(d, d ^ reach) for d in range(ways)])  7.45 us
    all_to_all x1, waiting for transfers between devices, body(): lax.all_to_all(send_dens, 'grid', split_axis=0, concat_axis=0, tiled=True)  6.35 us
    all_to_all x1, starting transfers between devices, body(): lax.all_to_all(send_energy, 'grid', split_axis=0, concat_axis=0, tiled=True)  6.12 us
    select_n x4, other arithmetic, gather_by_bits(): grown = jnp.where(here & reach == 0, mine_first, theirs_first)  5.87 us
    dot_general x1, matrix products, body(): jnp.einsum('rnw,mn->rmw', gathered.reshape(row_count, anc_count, width),...  5.64 us
  transfers between devices with their start and end apart: 7, of which 6 were waited for; matrix products, arithmetic and copies ran while one was open for 6% of the time, Pallas kernels for 0%

profile of v1, /device:TPU:0, one launch (start us, length us, event | category | flops | bytes accessed | tf_op | source)
XLA Modules:
  0.0 250.5 jit_solution(2468960225905282964)
XLA Ops:
  7.2 3.1 %collective-permute-start = (bf16[192,1536]{1,0:T(8,128)(2,1)}, bf16[192,1536]{1,0:T(8,128)(2,1)S(1)}, u32[]{:S(2)}, u32[]{:S(2)}) collective-permute-start(bf16[192,1536]{1,0:T(8,128)(2,1)} %bitcast.56), channel_id=1, source_target_pairs={{0,1},{1,0},{2,3},{3,2},{4,5},{5,4},{6,7},{7,6},{8,9},{9,8},{10,11... | collective-permute-start | bytes 1769480 | tf_op jit(solution)/shard_map/ppermute | solution.py:11
  10.3 1.4 copy.35
  11.6 12.2 %collective-permute-done = bf16[192,1536]{1,0:T(8,128)(2,1)S(1)} collective-permute-done((bf16[192,1536]{1,0:T(8,128)(2,1)}, bf16[192,1536]{1,0:T(8,128)(2,1)S(1)}, u32[]{:S(2)}, u32[]{:S(2)}) %collective-permute-start) | collective-permute-done | bytes 589856 | tf_op jit(solution)/shard_map/ppermute | solution.py:11
  25.5 1.9 collective-permute-start.1
  27.4 25.3 %collective-permute-done.1 = bf16[384,1536]{0,1:T(8,128)(2,1)S(1)} collective-permute-done((bf16[384,1536]{0,1:T(8,128)(2,1)S(1)}, bf16[384,1536]{0,1:T(8,128)(2,1)S(1)}, u32[]{:S(2)}, u32[]{:S(2)}) %collective-permute-start.1) | collective-permute-done | bytes 1179680 | tf_op jit(solution)/shard_map/ppermute | solution.py:11
  52.7 1.8 maximum_select_fusion.3
  54.5 2.5 %collective-permute-start.2 = (bf16[768,1536]{0,1:T(8,128)(2,1)}, bf16[768,1536]{0,1:T(8,128)(2,1)}, u32[]{:S(2)}, u32[]{:S(2)}) collective-permute-start(bf16[768,1536]{0,1:T(8,128)(2,1)} %maximum_select_fusion.3), channel_id=1, source_target_pairs={{0,4},{1,5},{2,6},{3,7},{4,0},{5,1},{6,2},{7,3},{8,12},{9,13},{10,... | collective-permute-start | bytes 7077896 | tf_op jit(solution)/shard_map/ppermute | solution.py:11
  60.5 1.7 concatenate.44
  62.9 2.3 copy.39
  65.2 2.6 %maximum_select_fusion.2 = bf16[768,6,256]{2,1,0:T(8,128)(2,1)} fusion(bf16[384,6,256]{2,1,0:T(8,128)(2,1)S(1)} %copy.39, bf16[384,6,256]{2,1,0:T(8,128)(2,1)S(1)} %maximum_select_fusion.6, pred[]{:T(512)S(6)} %eq.103), kind=kLoop, calls=%fused_computation.8 | loop fusion | flops 3538944 | bytes 4718593 | tf_op jit(solution)/shard_map/jit(_where)/select_n | solution.py:14
  67.7 90.1 %collective-permute-done.2 = bf16[768,1536]{0,1:T(8,128)(2,1)} collective-permute-done((bf16[768,1536]{0,1:T(8,128)(2,1)}, bf16[768,1536]{0,1:T(8,128)(2,1)}, u32[]{:S(2)}, u32[]{:S(2)}) %collective-permute-start.2) | collective-permute-done | bytes 2359328 | tf_op jit(solution)/shard_map/ppermute | solution.py:11
  157.8 5.1 %copy.41 = bf16[768,6,256]{2,1,0:T(8,128)(2,1)} copy(bf16[768,6,256]{0,2,1:T(8,128)(2,1)} %bitcast.9) | data formatting | bytes 4718592 | tf_op jit(solution)/shard_map/concatenate | solution.py:12
  162.9 5.6 %fusion.8 = bf16[1536,2,256]{2,1,0:T(2,128)(2,1)} fusion(bf16[768,6,256]{2,1,0:T(8,128)(2,1)} %copy.41, bf16[768,6,256]{2,1,0:T(8,128)(2,1)S(1)} %copy-done.1, pred[]{:T(512)S(6)} %eq.102, s32[2]{0:T(128)S(1)} %bitcast.62), kind=kOutput, calls=%fused_computation.13 | convolution fusion | flops 31457292 | bytes 6291465 | tf_op jit(solution)/shard_map/rnw,mn->rmw/dot_general | solution.py:40
  168.6 2.8 %reshape.106 = bf16[6,256,512]{2,1,0:T(8,128)(2,1)S(1)} reshape(bf16[1536,2,256]{2,1,0:T(2,128)(2,1)} %fusion.8) | data formatting | bytes 3145728 | tf_op jit(solution)/shard_map/reshape.46
  172.9 1.2 fusion.13
  174.1 1.3 fusion.10
  177.3 39.4 %psum.7 = f32[]{:T(128)} all-reduce(f32[]{:T(128)S(6)} %mul.94), channel_id=1, replica_groups=mesh['pole'=4,'grid'=8] {'pole','grid'}, use_global_device_ids=true, to_apply=%region_6.7 | all-reduce | flops 1 | bytes 8 | tf_op jit(solution)/shard_map/psum | solution.py:61
  216.7 1.1 convolution_convert_fusion.1
  218.7 6.1 %all-to-all-start.1 = ((bf16[8,32,192]{2,1,0:T(8,128)(2,1)}), bf16[8,32,192]{2,1,0:T(8,128)(2,1)S(1)}, u32[]{:S(2)}, u32[]{:S(2)}) async-start(bf16[8,32,192]{2,1,0:T(8,128)(2,1)} %bitcast.23), calls=%async_computation.3 | async-start | bytes 262144 | tf_op jit(solution)/shard_map/all_to_all | solution.py:92
  225.4 1.1 convolution_convert_fusion.3
  227.3 4.8 %all-to-all-done.1 = bf16[8,32,192]{2,1,0:T(8,128)(2,1)S(1)} async-done(((bf16[8,32,192]{2,1,0:T(8,128)(2,1)}), bf16[8,32,192]{2,1,0:T(8,128)(2,1)S(1)}, u32[]{:S(2)}, u32[]{:S(2)}) %all-to-all-start.1) | async-done | bytes 98336 | tf_op jit(solution)/shard_map/all_to_all | solution.py:92
  232.1 3.4 %all-to-all-start = ((bf16[8,32,192]{2,1,0:T(8,128)(2,1)}), bf16[8,32,192]{2,1,0:T(8,128)(2,1)S(1)}, u32[]{:S(2)}, u32[]{:S(2)}) async-start(bf16[8,32,192]{2,1,0:T(8,128)(2,1)} %bitcast.18), calls=%async_computation.1 | async-start | bytes 262144 | tf_op jit(solution)/shard_map/all_to_all | solution.py:91
  235.5 0.9 convolution_convert_fusion
  236.4 6.3 %all-to-all-done = bf16[8,32,192]{2,1,0:T(8,128)(2,1)S(1)} async-done(((bf16[8,32,192]{2,1,0:T(8,128)(2,1)}), bf16[8,32,192]{2,1,0:T(8,128)(2,1)S(1)}, u32[]{:S(2)}, u32[]{:S(2)}) %all-to-all-start) | async-done | bytes 98336 | tf_op jit(solution)/shard_map/all_to_all | solution.py:91
  (50 shorter events, 9.7 us)
Async XLA Ops:
  7.2 209.6 %reduce-scatter.5.cloned.1.call-start = ((), (), s32[]{:S(2)}) async-start(), calls=%async_computation.5 | async-start | bytes 983040 | tf_op jit(solution)/shard_map/reduce_scatter | solution.py:66
  7.2 16.6 %collective-permute-start = (bf16[192,1536]{1,0:T(8,128)(2,1)}, bf16[192,1536]{1,0:T(8,128)(2,1)S(1)}, u32[]{:S(2)}, u32[]{:S(2)}) collective-permute-start(bf16[192,1536]{1,0:T(8,128)(2,1)} %bitcast.56), channel_id=1, source_target_pairs={{0,1},{1,0},{2,3},{3,2},{4,5},{5,4},{6,7},{7,6},{8,9},{9,8},{10,11... | collective-permute-start | bytes 1769480 | tf_op jit(solution)/shard_map/ppermute | solution.py:11
  23.8 0.8 copy-start.3
  25.5 27.2 %collective-permute-start.1 = (bf16[384,1536]{0,1:T(8,128)(2,1)S(1)}, bf16[384,1536]{0,1:T(8,128)(2,1)S(1)}, u32[]{:S(2)}, u32[]{:S(2)}) collective-permute-start(bf16[384,1536]{0,1:T(8,128)(2,1)S(1)} %maximum_select_fusion.9), channel_id=1, source_target_pairs={{0,2},{1,3},{2,0},{3,1},{4,6},{5,7},{6,4},{7,5},{8,10},{9,11},{10,... | collective-permute-start | bytes 3538952 | tf_op jit(solution)/shard_map/ppermute | solution.py:11
  27.4 29.6 %copy-start.2 = (bf16[1,192,1536]{2,1,0:T(8,128)(2,1)S(1)}, bf16[1,192,1536]{2,1,0:T(8,128)(2,1)}, u32[]{:S(2)}) copy-start(bf16[1,192,1536]{2,1,0:T(8,128)(2,1)} %param.11) | copy-start | bytes 1769476
  27.4 32.2 %copy-start.10 = (s32[1,2]{1,0:T(1,128)S(1)}, s32[1,2]{1,0:T(1,128)}, u32[]{:S(2)}) copy-start(s32[1,2]{1,0:T(1,128)} %param.19) | copy-start | bytes 28
  27.4 32.3 %copy-start.11 = (s32[1,2]{1,0:T(1,128)S(1)}, s32[1,2]{1,0:T(1,128)}, u32[]{:S(2)}) copy-start(s32[1,2]{1,0:T(1,128)} %param.17) | copy-start | bytes 28
  27.4 32.3 %copy-start.4 = (bf16[1,1,2,256,256]{4,3,2,1,0:T(8,128)(2,1)S(1)}, bf16[1,1,2,256,256]{4,3,2,1,0:T(8,128)(2,1)}, u32[]{:S(2)}) copy-start(bf16[1,1,2,256,256]{4,3,2,1,0:T(8,128)(2,1)} %param.12) | copy-start | bytes 786436
  52.7 1.8 copy-start
  54.5 103.3 %collective-permute-start.2 = (bf16[768,1536]{0,1:T(8,128)(2,1)}, bf16[768,1536]{0,1:T(8,128)(2,1)}, u32[]{:S(2)}, u32[]{:S(2)}) collective-permute-start(bf16[768,1536]{0,1:T(8,128)(2,1)} %maximum_select_fusion.3), channel_id=1, source_target_pairs={{0,4},{1,5},{2,6},{3,7},{4,0},{5,1},{6,2},{7,3},{8,12},{9,13},{10,... | collective-permute-start | bytes 7077896 | tf_op jit(solution)/shard_map/ppermute | solution.py:11
  157.8 5.1 %copy-start.1 = (bf16[768,6,256]{2,1,0:T(8,128)(2,1)S(1)}, bf16[768,6,256]{2,1,0:T(8,128)(2,1)}, u32[]{:S(2)}) copy-start(bf16[768,6,256]{2,1,0:T(8,128)(2,1)} %maximum_select_fusion.2) | copy-start | bytes 7077892
  168.6 2.8 %copy-start.5 = (bf16[1,1,2,256,256]{4,3,2,1,0:T(8,128)(2,1)S(1)}, bf16[1,1,2,256,256]{4,3,2,1,0:T(8,128)(2,1)}, u32[]{:S(2)}) copy-start(bf16[1,1,2,256,256]{4,3,2,1,0:T(8,128)(2,1)} %broadcast_multiply_fusion) | copy-start | bytes 786436
  172.0 0.9 copy-start.6
  172.0 1.0 copy-start.7
  172.9 3.3 %copy-start.9 = (s32[256]{0:T(256)S(1)}, s32[256]{0:T(256)}, u32[]{:S(2)}) copy-start(s32[256]{0:T(256)} %param.20) | copy-start | bytes 3076
  172.9 3.5 %copy-start.8 = (s32[256]{0:T(256)S(1)}, s32[256]{0:T(256)}, u32[]{:S(2)}) copy-start(s32[256]{0:T(256)} %param.21) | copy-start | bytes 3076
  175.4 50.0 %reduce-scatter.3.cloned.1.call-start = ((), (), s32[]{:S(2)}) async-start(), calls=%async_computation.4 | async-start | bytes 983040 | tf_op jit(solution)/shard_map/reduce_scatter | solution.py:65
  218.7 13.5 %all-to-all-start.1 = ((bf16[8,32,192]{2,1,0:T(8,128)(2,1)}), bf16[8,32,192]{2,1,0:T(8,128)(2,1)S(1)}, u32[]{:S(2)}, u32[]{:S(2)}) async-start(bf16[8,32,192]{2,1,0:T(8,128)(2,1)} %bitcast.23), calls=%async_computation.3 | async-start | bytes 262144 | tf_op jit(solution)/shard_map/all_to_all | solution.py:92
  232.1 10.7 %all-to-all-start = ((bf16[8,32,192]{2,1,0:T(8,128)(2,1)}), bf16[8,32,192]{2,1,0:T(8,128)(2,1)S(1)}, u32[]{:S(2)}, u32[]{:S(2)}) async-start(bf16[8,32,192]{2,1,0:T(8,128)(2,1)} %bitcast.18), calls=%async_computation.1 | async-start | bytes 262144 | tf_op jit(solution)/shard_map/all_to_all | solution.py:91
Sparse Core Ops, SparseCore 0:
  175.6 24.0 reduce-scatter.4
  202.1 23.2 reduce-scatter.2
